TPU v7x, 32 devices: a whole 2x2x4 slice. The times are simulated.
32 devices in a mesh: mode: 8 (over z, x), row: 4 (over y, core).
Axes of the slice: x: 2, y: 2, z: 4, core: 2. Of those that a mesh axis runs over, the one named last changes fastest.
Arguments:
- forward: bfloat16 [64, 8, 2, 512], P('mode', 'row'), may hold values from -6 to 6
- backward: bfloat16 [64, 8, 2, 512], P('mode', 'row'), may hold values from -6 to 6
- propagator: bfloat16 [2, 512, 512], replicated, may hold values from -0.1875 to 0.1875
- row_taps: float32 [2, 3], replicated, may hold values from -3 to 3
- phase_masks: float32 [7, 8, 512], P(None, 'row'), may hold values from -3.140625 to 3.140625
- plane_index: int32 [4], replicated, may hold values from 0 to 6
- wave_ratio: float32 [4], replicated, may hold values from 0.7 to 1.4
- pair_list: int32 [80, 2], replicated, may hold values from 0 to 15, as said below
Outputs:
- coupling: float32 [2, 64, 64], P(None, 'mode')
- mask_grad: float32 [4, 8, 512], P(None, 'row')
Inputs may be any that keep to these rules, and one draw needn't show every extreme that they name: `pair_list`: each row names a target group and a forward group; no pair appears twice and every group is paired with itself; 80 pairs in all.
All inputs are finite; a program needn't handle non-finite values.
Results may differ from a plain program's by a relative error of at most 0.0078.
Values may be sent and summed in bfloat16 or wider, within the bound.
No kernel may reach another device: no remote copies, remote signals or barrier semaphores. Data moves between devices by JAX's collectives and lax.ppermute only.
A program may use at most 64 MiB of HBM per device.

v0:
```python
import math
import jax
import jax.numpy as jnp
from jax import lax
from jax.sharding import PartitionSpec as P

NG = 16


def padded_2(array, sides, width):
    for axis, dim in sides:
        peers, length = (lax.axis_size(axis), array.shape[dim])
        up = [(i, (i + 1) % peers) for i in range(peers - 1)]
        down = [(j, i) for i, j in up]
        last = lax.slice_in_dim(array, length - width, length, axis=dim)
        leading = lax.slice_in_dim(array, 0, width, axis=dim)
        before = lax.ppermute(last, axis, up)
        after = lax.ppermute(leading, axis, down)
        array = jnp.concatenate([before, array, after], axis=dim)
    return array


def chosen_phases(phase_masks, plane_index, wave_ratio):
    planes = jnp.arange(phase_masks.shape[0], dtype=jnp.int32)
    selector = (plane_index[:, None] == planes[None, :]).astype(jnp.float32)
    picked = jnp.einsum("wp,prc->wrc", selector, phase_masks, precision=lax.Precision.HIGHEST)
    return picked * wave_ratio[:, None, None]


def apply_mask(forward, phases):
    mode_total, row_total, _, width = forward.shape
    wave_total = phases.shape[0]
    shaped = forward.astype(jnp.float32).reshape(
        mode_total // wave_total, wave_total, row_total, 2, width
    )
    cosine = jnp.cos(phases)[None]
    sine = jnp.sin(phases)[None]
    real_part = shaped[:, :, :, 0] * cosine - shaped[:, :, :, 1] * sine
    imag_part = shaped[:, :, :, 0] * sine + shaped[:, :, :, 1] * cosine
    return jnp.stack([real_part, imag_part], axis=3).reshape(forward.shape).astype(jnp.bfloat16)


def forward_matrix(propagator):
    top_half = jnp.concatenate([propagator[0], propagator[1]], axis=1)
    low_half = jnp.concatenate([-propagator[1], propagator[0]], axis=1)
    return jnp.concatenate([top_half, low_half], axis=0)


def backward_matrix(propagator):
    top_half = jnp.concatenate([propagator[0].T, -propagator[1].T], axis=1)
    low_half = jnp.concatenate([propagator[1].T, propagator[0].T], axis=1)
    return jnp.concatenate([top_half, low_half], axis=0)


def propagate(fields, matrix):
    width = fields.shape[-1]
    result = jnp.dot(fields.reshape(-1, 2 * width), matrix, preferred_element_type=jnp.float32)
    return result.reshape(fields.shape)


def row_stencil(padded, row_taps, adjoint):
    values = padded.astype(jnp.float32)
    below_rows = values[:, :-2]
    center = values[:, 1:-1]
    above_rows = values[:, 2:]
    tap_real = row_taps[0]
    tap_imag = row_taps[1]
    if adjoint:
        sources = (above_rows, center, below_rows)
        tap_imag = -tap_imag
    else:
        sources = (below_rows, center, above_rows)
    real_sum = jnp.zeros(center[:, :, 0].shape, jnp.float32)
    imag_sum = jnp.zeros(center[:, :, 0].shape, jnp.float32)
    for position in range(3):
        source = sources[position]
        real_sum = (
            real_sum + tap_real[position] * source[:, :, 0] - tap_imag[position] * source[:, :, 1]
        )
        imag_sum = (
            imag_sum + tap_real[position] * source[:, :, 1] + tap_imag[position] * source[:, :, 0]
        )
    return jnp.stack([real_sum, imag_sum], axis=2)


def times_i(fields):
    return jnp.stack([-fields[:, :, 1], fields[:, :, 0]], axis=2)


def times_minus_i(fields):
    return jnp.stack([fields[:, :, 1], -fields[:, :, 0]], axis=2)


def body(forward, backward, propagator, row_taps, phase_masks, plane_index, wave_ratio, pair_list):
    local_modes, local_rows, _, width = forward.shape
    wave_total = wave_ratio.shape[0]
    mode_total = local_modes * lax.axis_size("mode")
    row_total = local_rows * lax.axis_size("row")
    group_size = mode_total // NG
    phases = chosen_phases(phase_masks, plane_index, wave_ratio)
    masked = apply_mask(forward, phases)
    spread = propagate(masked, forward_matrix(propagator)).astype(jnp.bfloat16)
    padded = padded_2(spread, (("row", 1),), 1)
    field = row_stencil(padded, row_taps, False).astype(jnp.bfloat16)
    field_flat = field.reshape(local_modes, -1)
    field_turned = times_minus_i(field).reshape(local_modes, -1)
    group_ids = jnp.arange(NG, dtype=jnp.int32)
    hits = (pair_list[:, 0][:, None, None] == group_ids[None, :, None]) & (
        pair_list[:, 1][:, None, None] == group_ids[None, None, :]
    )
    pair_matrix = jnp.sum(hits.astype(jnp.float32), axis=0)
    own_modes = lax.axis_index("mode") * local_modes + jnp.arange(local_modes, dtype=jnp.int32)
    own_onehot = ((own_modes // group_size)[:, None] == group_ids[None, :]).astype(jnp.float32)
    target_groups = jnp.arange(mode_total, dtype=jnp.int32) // group_size
    target_onehot = (target_groups[:, None] == group_ids[None, :]).astype(jnp.float32)
    own_pairs = jnp.dot(own_onehot, pair_matrix.T, precision=lax.Precision.HIGHEST)
    column_mask = jnp.dot(own_pairs, target_onehot.T, precision=lax.Precision.HIGHEST)
    shard_rows = lax.all_gather(backward, "mode", axis=0, tiled=True)
    rows_flat = shard_rows.reshape(shard_rows.shape[0], -1)
    real_part = jnp.einsum("nd,kd->nk", field_flat, rows_flat, preferred_element_type=jnp.float32)
    imag_part = jnp.einsum("nd,kd->nk", field_turned, rows_flat, preferred_element_type=jnp.float32)
    block = jnp.stack([real_part, imag_part])
    match_sum = lax.psum(block, "row")
    coupling = match_sum * (1.0 / math.sqrt(row_total * width)) * column_mask[None, :, :]
    weights = coupling.astype(jnp.bfloat16)
    shard_rows = lax.all_gather(backward, "mode", axis=0, tiled=True)
    row_count = shard_rows.shape[0]
    rows_flat = shard_rows.reshape(row_count, -1)
    rows_turned = times_i(shard_rows).reshape(row_count, -1)
    weight_real = weights[0]
    weight_imag = weights[1]
    running = jnp.dot(weight_real, rows_flat, preferred_element_type=jnp.float32)
    gathered = running + jnp.dot(weight_imag, rows_turned, preferred_element_type=jnp.float32)
    gathered = (
        (gathered * (1.0 / math.sqrt(mode_total))).astype(jnp.bfloat16).reshape(forward.shape)
    )
    padded_back = padded_2(gathered, (("row", 1),), 1)
    pulled = row_stencil(padded_back, row_taps, True).astype(jnp.bfloat16)
    adjoint = propagate(pulled, backward_matrix(propagator))
    masked_float = masked.astype(jnp.float32)
    term = masked_float[:, :, 1] * adjoint[:, :, 0] - masked_float[:, :, 0] * adjoint[:, :, 1]
    partial_grad = jnp.sum(
        term.reshape(local_modes // wave_total, wave_total, local_rows, width), axis=0
    )
    summed = lax.psum(partial_grad, "mode")
    mask_grad = summed * (-2.0 / math.sqrt(mode_total))
    return (coupling, mask_grad)


def solution(mesh):
    in_specs = (
        P("mode", "row", None, None),
        P("mode", "row", None, None),
        P(),
        P(),
        P(None, "row", None),
        P(),
        P(),
        P(),
    )
    out_specs = (P(None, "mode", None), P(None, "row", None))
    return jax.shard_map(body, mesh=mesh, in_specs=in_specs, out_specs=out_specs, check_vma=False)
```

profile of v0, /device:TPU:0, one launch (start us, length us, event | category | flops | bytes accessed | tf_op | source)
XLA Modules:
  0.0 117.6 jit_solution(7645582533571077190)
XLA Ops:
  0.6 0.0 copy-start
  0.6 0.0 copy-start.1
  0.7 0.0 copy-start.2
  0.7 0.0 copy-start.7
  0.7 0.0 copy-start.6
  0.7 2.7 %slice_bitcast_fusion = (bf16[512,512]{0,1:T(8,128)(2,1)}, bf16[512,512]{0,1:T(8,128)(2,1)}, bf16[512,512]{1,0:T(8,128)(2,1)}, bf16[512,512]{1,0:T(8,128)(2,1)}) fusion(bf16[2,512,512]{2,1,0:T(8,128)(2,1)} %param.10), kind=kLoop, calls=%fused_computation.10 | loop fusion | bytes 3145728 | tf_op jit(solution)/shard_map/transpose | solution.py:50
  3.4 0.0 copy-done.1
  3.4 0.9 fusion.19
  4.3 0.0 copy-done.2
  4.3 0.0 copy-done
  4.4 0.0 copy-done.7
  4.4 0.0 copy-done.6
  4.4 0.3 fusion.26
  4.8 1.8 %maximum_bitcast_fusion = bf16[1024,1024]{0,1:T(8,128)(2,1)S(1)} fusion(bf16[512,512]{1,0:T(8,128)(2,1)} %get-tuple-element.13, bf16[512,512]{1,0:T(8,128)(2,1)} %fusion.19, bf16[512,512]{1,0:T(8,128)(2,1)} %get-tuple-element.12), kind=kLoop, calls=%fused_computation.3 | loop fusion | flops 8388608 | bytes 3670016 | tf_op jit(solution)/shard_map/dot_general | solution.py:57
  6.6 2.6 %copy.33 = bf16[1024,1024]{1,0:T(8,128)(2,1)} copy(bf16[1024,1024]{0,1:T(8,128)(2,1)S(1)} %maximum_bitcast_fusion) | data formatting | bytes 4194304 | tf_op jit(solution)/shard_map/dot_general | solution.py:57
  9.2 0.0 copy-start.3
  9.2 0.0 copy-start.5
  9.2 0.0 copy-start.4
  9.2 2.3 %convolution_convert_fusion = bf16[8,2,2,512]{3,0,2,1:T(8,128)(2,1)S(1)} fusion(bf16[8,2,1024,1]{2,0,3,1:T(8,128)(2,1)S(1)} %bitcast.95, bf16[2,512,1024,1]{2,1,0,3:T(8,128)(2,1)} %bitcast.92), kind=kOutput, calls=%fused_computation.5 | convolution fusion | flops 33570816 | bytes 2162688 | tf_op jit(solution)/shard_map/dot_general | solution.py:57
  11.5 2.4 %collective-permute-start = (bf16[8,1,2,512]{3,0,2,1:T(8,128)(2,1)S(1)}, bf16[8,1,2,512]{3,0,2,1:T(8,128)(2,1)S(1)}, u32[]{:S(2)}, u32[]{:S(2)}) collective-permute-start(bf16[8,1,2,512]{3,0,2,1:T(8,128)(2,1)S(1)} %get-tuple-element.22), channel_id=1, source_target_pairs={{0,1},{1,2},{2,3},{4,5},{5,6},{6,7},{8,9},{9,10},{10,11},{12,13},{... | collective-permute-start | bytes 49160 | tf_op jit(solution)/shard_map/ppermute | solution.py:17
  13.9 1.3 %collective-permute-start.1 = (bf16[8,1,2,512]{3,0,2,1:T(8,128)(2,1)S(1)}, bf16[8,1,2,512]{3,0,2,1:T(8,128)(2,1)S(1)}, u32[]{:S(2)}, u32[]{:S(2)}) collective-permute-start(bf16[8,1,2,512]{3,0,2,1:T(8,128)(2,1)S(1)} %get-tuple-element.23), channel_id=1, source_target_pairs={{1,0},{2,1},{3,2},{5,4},{6,5},{7,6},{9,8},{10,9},{11,10},{13,12},{... | collective-permute-start | bytes 49160 | tf_op jit(solution)/shard_map/ppermute | solution.py:18
  15.2 0.8 fusion.20
  16.0 0.0 copy-done.3
  16.0 31.9 %all_gather.4 = bf16[64,2,2,512]{3,0,2,1:T(8,128)(2,1)S(1)} all-gather(bf16[8,2,2,512]{3,0,2,1:T(8,128)(2,1)S(1)} %copy.34), channel_id=1, replica_groups=mesh['mode'=8,'row'=4] {'mode'}, dimensions={0}, use_global_device_ids=true | all-gather | bytes 294912 | tf_op jit(solution)/shard_map/all_gather | solution.py:118
  47.9 0.0 copy-done.5
  48.0 0.0 copy-done.4
  48.0 0.1 convert_reduce_fusion
  48.1 0.2 fusion.11
  48.3 0.2 convolution_multiply_fusion.1
  48.5 0.1 pad_maximum_fusion
  48.6 1.8 %maximum_maximum_fusion = bf16[1024,1024]{0,1:T(8,128)(2,1)S(1)} fusion(bf16[512,512]{0,1:T(8,128)(2,1)} %get-tuple-element.11, bf16[512,512]{0,1:T(8,128)(2,1)} %get-tuple-element.10, bf16[512,512]{0,1:T(8,128)(2,1)} %fusion.20), kind=kLoop, calls=%fused_computation.4 | loop fusion | flops 8388608 | bytes 3670016 | tf_op jit(solution)/shard_map/concatenate | solution.py:52
  50.4 0.7 fusion.27
  51.0 0.3 copy.35
  51.3 0.2 reshape.169
  51.5 0.3 copy.36
  51.8 0.2 reshape.170
  52.0 0.0 collective-permute-done
  52.0 0.0 collective-permute-done.1
  52.0 3.7 %fusion.22 = (bf16[8,2,1,512]{3,0,2,1:T(8,128)(2,1)S(1)}, bf16[8,2,1,512]{3,0,2,1:T(8,128)(2,1)S(1)}) fusion(f32[8,4,2,512]{3,0,2,1:T(8,128)S(1)} %maximum_convert_fusion, f32[]{:T(128)} %bitcast.16, f32[]{:T(128)} %bitcast.15, f32[]{:T(128)} %bitcast.14, f32[]{:T(128)} %bitcast.13, f32[]{:T(128)} %bitcast.12, f32[]{:T(128)} %bitcast), kind=kLoop, calls=%fused_computation.70 | loop fusion | flops 106496 | bytes 229400 | tf_op jit(solution)/shard_map/neg | solution.py:91
  55.7 3.7 %add_convert_fusion.1 = bf16[8,2,1,512]{3,0,2,1:T(8,128)(2,1)S(1)} fusion(f32[8,4,2,512]{3,0,2,1:T(8,128)S(1)} %maximum_convert_fusion, f32[]{:T(128)} %bitcast.16, f32[]{:T(128)} %bitcast.15, f32[]{:T(128)} %bitcast.14, f32[]{:T(128)} %bitcast.13, f32[]{:T(128)} %bitcast.12, f32[]{:T(128)} %bitcast), kind=kLoop, calls=%fused_computation.33 | loop fusion | flops 98304 | bytes 213016 | tf_op jit(solution)/shard_map/slice | solution.py:91
  59.5 0.2 convolution_bitcast_fusion.1
  59.7 0.2 convolution_bitcast_fusion
  59.8 7.7 %psum.14 = f32[2,8,64]{2,1,0:T(8,128)S(1)} all-reduce(f32[2,8,64]{2,1,0:T(8,128)S(1)} %pad_maximum_fusion.2), channel_id=1, replica_groups=mesh['mode'=8,'row'=4] {'row'}, use_global_device_ids=true, to_apply=%region_0.0 | all-reduce | flops 1024 | bytes 8192 | tf_op jit(solution)/shard_map/psum | solution.py:123
  67.6 0.6 fusion.21
  68.2 0.1 fusion.12
  68.3 0.2 fusion.1
  68.5 2.3 %collective-permute-start.2 = (bf16[8,1,2,512]{3,0,2,1:T(8,128)(2,1)S(1)}, bf16[8,1,2,512]{3,0,2,1:T(8,128)(2,1)S(1)}, u32[]{:S(2)}, u32[]{:S(2)}) collective-permute-start(bf16[8,1,2,512]{3,0,2,1:T(8,128)(2,1)S(1)} %get-tuple-element.20), channel_id=1, source_target_pairs={{0,1},{1,2},{2,3},{4,5},{5,6},{6,7},{8,9},{9,10},{10,11},{12,13},{... | collective-permute-start | bytes 49160 | tf_op jit(solution)/shard_map/ppermute | solution.py:17
  70.8 1.3 %collective-permute-start.3 = (bf16[8,1,2,512]{3,0,2,1:T(8,128)(2,1)S(1)}, bf16[8,1,2,512]{3,0,2,1:T(8,128)(2,1)S(1)}, u32[]{:S(2)}, u32[]{:S(2)}) collective-permute-start(bf16[8,1,2,512]{3,0,2,1:T(8,128)(2,1)S(1)} %get-tuple-element.21), channel_id=1, source_target_pairs={{1,0},{2,1},{3,2},{5,4},{6,5},{7,6},{9,8},{10,9},{11,10},{13,12},{... | collective-permute-start | bytes 49160 | tf_op jit(solution)/shard_map/ppermute | solution.py:18
  72.1 0.7 fusion.28
  72.8 0.0 collective-permute-done.2
  72.8 2.6 %collective-permute-done.3 = bf16[8,1,2,512]{3,0,2,1:T(8,128)(2,1)S(1)} collective-permute-done((bf16[8,1,2,512]{3,0,2,1:T(8,128)(2,1)S(1)}, bf16[8,1,2,512]{3,0,2,1:T(8,128)(2,1)S(1)}, u32[]{:S(2)}, u32[]{:S(2)}) %collective-permute-start.3) | collective-permute-done | bytes 16416 | tf_op jit(solution)/shard_map/ppermute | solution.py:18
  75.4 3.8 %subtract_convert_fusion = (bf16[8,2,1,512]{3,0,2,1:T(8,128)(2,1)S(1)}, bf16[8,2,1,512]{3,0,2,1:T(8,128)(2,1)S(1)}) fusion(f32[8,4,2,512]{3,0,2,1:T(8,128)S(1)} %maximum_convert_fusion.1, f32[]{:T(128)} %bitcast.30, f32[]{:T(128)} %bitcast.29, f32[]{:T(128)} %bitcast.28, f32[]{:T(128)} %bitcast.15, f32[]{:T(128)} %bitcast.13, f32[]{:T(128)} %bitcast), kind=kLoop, calls=%fused_computation.31 | loop fusion | flops 196608 | bytes 229400 | tf_op jit(solution)/shard_map/convert.1
  79.2 0.6 fusion.29
  79.9 37.1 %psum.15 = f32[4,2,512]{2,0,1:T(4,128)S(1)} all-reduce(f32[4,2,512]{2,0,1:T(4,128)S(1)} %reduce_sum.19), channel_id=1, replica_groups=mesh['mode'=8,'row'=4] {'mode'}, use_global_device_ids=true, to_apply=%region_3.4 | all-reduce | flops 4096 | bytes 32768 | tf_op jit(solution)/shard_map/psum | solution.py:145
  117.0 0.6 copy.37
  (24 shorter events, 0.3 us)
Async XLA Ops:
  0.6 3.7 %copy-start = (f32[7,2,512]{2,1,0:T(2,128)S(1)}, f32[7,2,512]{2,1,0:T(2,128)}, u32[]{:S(2)}) copy-start(f32[7,2,512]{2,1,0:T(2,128)} %param.12) | copy-start | bytes 86020
  0.6 2.8 %copy-start.1 = (bf16[2,512,512]{2,1,0:T(8,128)(2,1)S(1)}, bf16[2,512,512]{2,1,0:T(8,128)(2,1)}, u32[]{:S(2)}) copy-start(bf16[2,512,512]{2,1,0:T(8,128)(2,1)} %param.10) | copy-start | bytes 3145732
  0.7 3.6 %copy-start.2 = (bf16[8,2,2,512]{3,2,1,0:T(2,128)(2,1)S(1)}, bf16[8,2,2,512]{3,2,1,0:T(2,128)(2,1)}, u32[]{:S(2)}) copy-start(bf16[8,2,2,512]{3,2,1,0:T(2,128)(2,1)} %param.8) | copy-start | bytes 98308
  0.7 3.7 %copy-start.7 = (s32[4]{0:T(128)S(1)}, s32[4]{0:T(128)}, u32[]{:S(2)}) copy-start(s32[4]{0:T(128)} %param.13) | copy-start | bytes 52
  0.7 3.7 %copy-start.6 = (f32[4]{0:T(128)S(1)}, f32[4]{0:T(128)}, u32[]{:S(2)}) copy-start(f32[4]{0:T(128)} %param.14) | copy-start | bytes 52
  9.2 6.8 %copy-start.3 = (bf16[8,2,2,512]{3,2,1,0:T(2,128)(2,1)S(1)}, bf16[8,2,2,512]{3,2,1,0:T(2,128)(2,1)}, u32[]{:S(2)}) copy-start(bf16[8,2,2,512]{3,2,1,0:T(2,128)(2,1)} %param.9) | copy-start | bytes 98308
  9.2 38.7 %copy-start.5 = (s32[80,2]{0,1:T(2,128)S(1)}, s32[80,2]{0,1:T(2,128)}, u32[]{:S(2)}) copy-start(s32[80,2]{0,1:T(2,128)} %param.15) | copy-start | bytes 1924
  9.2 38.8 %copy-start.4 = (f32[2,3]{1,0:T(2,128)S(1)}, f32[2,3]{1,0:T(2,128)}, u32[]{:S(2)}) copy-start(f32[2,3]{1,0:T(2,128)} %param.11) | copy-start | bytes 76
  11.5 40.5 %collective-permute-start = (bf16[8,1,2,512]{3,0,2,1:T(8,128)(2,1)S(1)}, bf16[8,1,2,512]{3,0,2,1:T(8,128)(2,1)S(1)}, u32[]{:S(2)}, u32[]{:S(2)}) collective-permute-start(bf16[8,1,2,512]{3,0,2,1:T(8,128)(2,1)S(1)} %get-tuple-element.22), channel_id=1, source_target_pairs={{0,1},{1,2},{2,3},{4,5},{5,6},{6,7},{8,9},{9,10},{10,11},{12,13},{... | collective-permute-start | bytes 49160 | tf_op jit(solution)/shard_map/ppermute | solution.py:17
  13.9 38.1 %collective-permute-start.1 = (bf16[8,1,2,512]{3,0,2,1:T(8,128)(2,1)S(1)}, bf16[8,1,2,512]{3,0,2,1:T(8,128)(2,1)S(1)}, u32[]{:S(2)}, u32[]{:S(2)}) collective-permute-start(bf16[8,1,2,512]{3,0,2,1:T(8,128)(2,1)S(1)} %get-tuple-element.23), channel_id=1, source_target_pairs={{1,0},{2,1},{3,2},{5,4},{6,5},{7,6},{9,8},{10,9},{11,10},{13,12},{... | collective-permute-start | bytes 49160 | tf_op jit(solution)/shard_map/ppermute | solution.py:18
  68.5 4.2 %collective-permute-start.2 = (bf16[8,1,2,512]{3,0,2,1:T(8,128)(2,1)S(1)}, bf16[8,1,2,512]{3,0,2,1:T(8,128)(2,1)S(1)}, u32[]{:S(2)}, u32[]{:S(2)}) collective-permute-start(bf16[8,1,2,512]{3,0,2,1:T(8,128)(2,1)S(1)} %get-tuple-element.20), channel_id=1, source_target_pairs={{0,1},{1,2},{2,3},{4,5},{5,6},{6,7},{8,9},{9,10},{10,11},{12,13},{... | collective-permute-start | bytes 49160 | tf_op jit(solution)/shard_map/ppermute | solution.py:17
  70.8 4.6 %collective-permute-start.3 = (bf16[8,1,2,512]{3,0,2,1:T(8,128)(2,1)S(1)}, bf16[8,1,2,512]{3,0,2,1:T(8,128)(2,1)S(1)}, u32[]{:S(2)}, u32[]{:S(2)}) collective-permute-start(bf16[8,1,2,512]{3,0,2,1:T(8,128)(2,1)S(1)} %get-tuple-element.21), channel_id=1, source_target_pairs={{1,0},{2,1},{3,2},{5,4},{6,5},{7,6},{9,8},{10,9},{11,10},{13,12},{... | collective-permute-start | bytes 49160 | tf_op jit(solution)/shard_map/ppermute | solution.py:18
where the time goes:
time: 118 us
  blocking collectives  76.7 us (65%)
  other arithmetic  17.5 us (15%)
  local copies, waits for them, and re-layouts  8.32 us (7%)
  starting transfers between devices  7.2 us (6%)
  matrix products  4.26 us (4%)
  waiting for transfers between devices  2.63 us (2%)
    psum x1, blocking collectives, body(): summed = lax.psum(partial_grad, 'mode')  37.1 us
    all_gather x1, blocking collectives, body(): shard_rows = lax.all_gather(backward, 'mode', axis=0, tiled=True)  31.9 us
    psum x1, blocking collectives, body(): match_sum = lax.psum(block, 'row')  7.74 us
    ppermute x2, starting transfers between devices, padded_2(): before = lax.ppermute(last, axis, up)  4.61 us
    another operation x2, other arithmetic  3.81 us
    neg x1, other arithmetic, times_minus_i(): return jnp.stack([fields[:, :, 1], -fields[:, :, 0]], axis=2)  3.74 us
    slice x1, other arithmetic, times_minus_i(): return jnp.stack([fields[:, :, 1], -fields[:, :, 0]], axis=2)  3.74 us
    dot_general x2, matrix products, propagate(): jnp.dot(fields.reshape(-1, 2 * width), matrix, preferred_element_type=jnp...  2.92 us
  transfers between devices with their start and end apart: 4, of which 1 were waited for; matrix products, arithmetic and copies ran while one was open for 5% of the time, Pallas kernels for 0%

commit v1 on v0

--- a/solution.py
+++ b/solution.py
@@ -142,7 +142,8 @@
     partial_grad = jnp.sum(
         term.reshape(local_modes // wave_total, wave_total, local_rows, width), axis=0
     )
-    summed = lax.psum(partial_grad, "mode")
+    parts = lax.all_gather(partial_grad, "mode", axis=0, tiled=False)
+    summed = parts.sum(axis=0)
     mask_grad = summed * (-2.0 / math.sqrt(mode_total))
     return (coupling, mask_grad)
 

time: 118 us -> 114 us (0.966)
  blocking collectives: 76.7 us -> 70.2 us
    psum x1 -> x0, blocking collectives: 37.1 us -> none  [body(): summed = lax.psum(partial_grad, 'mode')]
    all_gather x0 -> x1, blocking collectives: none -> 30.5 us  [body(): parts = lax.all_gather(partial_grad, 'mode', axis=0, tiled=False)]
  transfers between devices with their start and end apart: 4 -> 4, of which waited for: 1 -> 1; matrix products, arithmetic and copies ran while one was open for 5% -> 6% of each run, Pallas kernels for 0% -> 0%
where the time goes in v1:
time: 114 us; the launch traced here: 113 us
  blocking collectives  70.2 us (62%)
  other arithmetic  18.1 us (16%)
  local copies, waits for them, and re-layouts  9.32 us (8%)
  starting transfers between devices  7.19 us (6%)
  matrix products  4.93 us (4%)
  waiting for transfers between devices  2.62 us (2%)
    all_gather x1, blocking collectives, body(): shard_rows = lax.all_gather(backward, 'mode', axis=0, tiled=True)  31.9 us
    all_gather x1, blocking collectives, body(): parts = lax.all_gather(partial_grad, 'mode', axis=0, tiled=False)  30.5 us
    psum x1, blocking collectives, body(): match_sum = lax.psum(block, 'row')  7.74 us
    ppermute x2, starting transfers between devices, padded_2(): before = lax.ppermute(last, axis, up)  4.6 us
    another operation x2, other arithmetic  3.76 us
    neg x1, other arithmetic, times_minus_i(): return jnp.stack([fields[:, :, 1], -fields[:, :, 0]], axis=2)  3.72 us
    slice x1, other arithmetic, times_minus_i(): return jnp.stack([fields[:, :, 1], -fields[:, :, 0]], axis=2)  3.71 us
    dot_general x2, matrix products, propagate(): jnp.dot(fields.reshape(-1, 2 * width), matrix, preferred_element_type=jnp...  2.94 us
  transfers between devices with their start and end apart: 4, of which 1 were waited for; matrix products, arithmetic and copies ran while one was open for 6% of the time, Pallas kernels for 0%

profile of v1, /device:TPU:0, one launch (start us, length us, event | category | flops | bytes accessed | tf_op | source)
XLA Modules:
  0.0 113.4 jit_solution(6418136034371616115)
XLA Ops:
  0.6 0.0 copy-start
  0.6 0.0 copy-start.1
  0.7 0.0 copy-start.3
  0.7 0.0 copy-start.10
  0.7 0.0 copy-start.9
  0.7 2.7 %slice_bitcast_fusion = (bf16[512,512]{0,1:T(8,128)(2,1)}, bf16[512,512]{0,1:T(8,128)(2,1)}, bf16[512,512]{1,0:T(8,128)(2,1)}, bf16[512,512]{1,0:T(8,128)(2,1)}) fusion(bf16[2,512,512]{2,1,0:T(8,128)(2,1)} %param.10), kind=kLoop, calls=%fused_computation.10 | loop fusion | bytes 3145728 | tf_op jit(solution)/shard_map/transpose | solution.py:50
  3.4 0.0 copy-done.1
  3.4 0.9 fusion.19
  4.3 0.0 copy-done.3
  4.3 0.0 copy-done
  4.3 0.0 copy-done.10
  4.3 0.0 copy-done.9
  4.4 0.3 fusion.26
  4.8 1.8 %maximum_bitcast_fusion = bf16[1024,1024]{0,1:T(8,128)(2,1)S(1)} fusion(bf16[512,512]{1,0:T(8,128)(2,1)} %get-tuple-element.9, bf16[512,512]{1,0:T(8,128)(2,1)} %fusion.19, bf16[512,512]{1,0:T(8,128)(2,1)} %get-tuple-element.8), kind=kLoop, calls=%fused_computation.3 | loop fusion | flops 8388608 | bytes 3670016 | tf_op jit(solution)/shard_map/dot_general | solution.py:57
  6.6 2.6 %copy.33 = bf16[1024,1024]{1,0:T(8,128)(2,1)} copy(bf16[1024,1024]{0,1:T(8,128)(2,1)S(1)} %maximum_bitcast_fusion) | data formatting | bytes 4194304 | tf_op jit(solution)/shard_map/dot_general | solution.py:57
  9.2 0.0 copy-start.4
  9.2 0.0 copy-start.8
  9.2 0.0 copy-start.5
  9.2 0.0 copy-start.2
  9.2 2.3 %convolution_convert_fusion = bf16[8,2,2,512]{3,0,2,1:T(8,128)(2,1)S(1)} fusion(bf16[8,2,1024,1]{2,0,3,1:T(8,128)(2,1)S(1)} %bitcast.97, bf16[2,512,1024,1]{2,1,0,3:T(8,128)(2,1)} %bitcast.93), kind=kOutput, calls=%fused_computation.5 | convolution fusion | flops 33570816 | bytes 2162688 | tf_op jit(solution)/shard_map/dot_general | solution.py:57
  11.5 0.6 fusion.24
  12.1 2.3 %collective-permute-start = (bf16[8,1,2,512]{3,0,2,1:T(8,128)(2,1)}, bf16[8,1,2,512]{3,0,2,1:T(8,128)(2,1)S(1)}, u32[]{:S(2)}, u32[]{:S(2)}) collective-permute-start(bf16[8,1,2,512]{3,0,2,1:T(8,128)(2,1)} %get-tuple-element.18), channel_id=1, source_target_pairs={{0,1},{1,2},{2,3},{4,5},{5,6},{6,7},{8,9},{9,10},{10,11},{12,13},{... | collective-permute-start | bytes 49160 | tf_op jit(solution)/shard_map/ppermute | solution.py:17
  14.5 1.3 %collective-permute-start.1 = (bf16[8,1,2,512]{3,0,2,1:T(8,128)(2,1)S(1)}, bf16[8,1,2,512]{3,0,2,1:T(8,128)(2,1)S(1)}, u32[]{:S(2)}, u32[]{:S(2)}) collective-permute-start(bf16[8,1,2,512]{3,0,2,1:T(8,128)(2,1)S(1)} %get-tuple-element.19), channel_id=1, source_target_pairs={{1,0},{2,1},{3,2},{5,4},{6,5},{7,6},{9,8},{10,9},{11,10},{13,12},{... | collective-permute-start | bytes 49160 | tf_op jit(solution)/shard_map/ppermute | solution.py:18
  15.8 0.0 copy-done.4
  15.9 31.9 %all_gather.10 = bf16[64,2,2,512]{3,0,2,1:T(8,128)(2,1)S(1)} all-gather(bf16[8,2,2,512]{3,0,2,1:T(8,128)(2,1)S(1)} %copy.34), channel_id=1, replica_groups=mesh['mode'=8,'row'=4] {'mode'}, dimensions={0}, use_global_device_ids=true | all-gather | bytes 294912 | tf_op jit(solution)/shard_map/all_gather | solution.py:118
  47.8 0.0 copy-done.8
  47.8 0.0 copy-done.5
  47.8 0.6 slice_negate_fusion.1
  48.4 0.1 convert_reduce_fusion
  48.5 0.2 fusion.11
  48.7 0.8 convolution_multiply_fusion.1
  49.5 0.7 pad_maximum_fusion
  50.3 0.0 copy-done.2
  50.3 1.5 %maximum_maximum_fusion = bf16[1024,1024]{0,1:T(8,128)(2,1)S(1)} fusion(bf16[512,512]{0,1:T(8,128)(2,1)} %get-tuple-element.7, bf16[512,512]{0,1:T(8,128)(2,1)S(1)} %copy-done.2, bf16[512,512]{0,1:T(8,128)(2,1)S(1)} %fusion.20), kind=kLoop, calls=%fused_computation.4 | loop fusion | flops 8388608 | bytes 3670016 | tf_op jit(solution)/shard_map/concatenate | solution.py:52
  51.7 0.0 copy-start.7
  51.7 0.0 copy-start.6
  51.8 0.7 fusion.27
  52.4 0.3 copy.35
  52.7 0.2 reshape.169
  52.9 1.2 %copy.36 = bf16[64,2,2,512]{3,2,1,0:T(2,128)(2,1)S(1)} copy(bf16[64,2,2,512]{3,0,2,1:T(8,128)(2,1)} %pad_maximum_fusion) | data formatting | bytes 524288 | tf_op jit(solution)/shard_map/stack | solution.py:87
  54.1 0.2 reshape.170
  54.3 0.0 collective-permute-done
  54.3 0.0 collective-permute-done.1
  54.3 3.7 %fusion.22 = (bf16[8,2,1,512]{3,0,2,1:T(8,128)(2,1)S(1)}, bf16[8,2,1,512]{3,0,2,1:T(8,128)(2,1)S(1)}) fusion(f32[8,4,2,512]{3,0,2,1:T(8,128)S(1)} %maximum_convert_fusion, f32[]{:T(128)} %bitcast.16, f32[]{:T(128)} %bitcast.15, f32[]{:T(128)} %bitcast.14, f32[]{:T(128)} %bitcast.13, f32[]{:T(128)} %bitcast.12, f32[]{:T(128)} %bitcast), kind=kLoop, calls=%fused_computation.70 | loop fusion | flops 106496 | bytes 229400 | tf_op jit(solution)/shard_map/neg | solution.py:91
  58.1 3.7 %add_convert_fusion.1 = bf16[8,2,1,512]{3,0,2,1:T(8,128)(2,1)S(1)} fusion(f32[8,4,2,512]{3,0,2,1:T(8,128)S(1)} %maximum_convert_fusion, f32[]{:T(128)} %bitcast.16, f32[]{:T(128)} %bitcast.15, f32[]{:T(128)} %bitcast.14, f32[]{:T(128)} %bitcast.13, f32[]{:T(128)} %bitcast.12, f32[]{:T(128)} %bitcast), kind=kLoop, calls=%fused_computation.33 | loop fusion | flops 98304 | bytes 213016 | tf_op jit(solution)/shard_map/slice | solution.py:91
  61.8 0.2 convolution_bitcast_fusion.1
  61.9 0.2 convolution_bitcast_fusion
  62.1 7.7 %psum.7 = f32[2,8,64]{2,1,0:T(8,128)S(1)} all-reduce(f32[2,8,64]{2,1,0:T(8,128)S(1)} %pad_maximum_fusion.2), channel_id=1, replica_groups=mesh['mode'=8,'row'=4] {'row'}, use_global_device_ids=true, to_apply=%region_0.0 | all-reduce | flops 1024 | bytes 8192 | tf_op jit(solution)/shard_map/psum | solution.py:123
  69.9 0.0 copy-done.7
  69.9 0.6 fusion.21
  70.5 0.1 fusion.12
  70.6 0.2 fusion.1
  70.8 2.3 %collective-permute-start.2 = (bf16[8,1,2,512]{3,0,2,1:T(8,128)(2,1)S(1)}, bf16[8,1,2,512]{3,0,2,1:T(8,128)(2,1)S(1)}, u32[]{:S(2)}, u32[]{:S(2)}) collective-permute-start(bf16[8,1,2,512]{3,0,2,1:T(8,128)(2,1)S(1)} %get-tuple-element.16), channel_id=1, source_target_pairs={{0,1},{1,2},{2,3},{4,5},{5,6},{6,7},{8,9},{9,10},{10,11},{12,13},{... | collective-permute-start | bytes 49160 | tf_op jit(solution)/shard_map/ppermute | solution.py:17
  73.1 1.3 %collective-permute-start.3 = (bf16[8,1,2,512]{3,0,2,1:T(8,128)(2,1)S(1)}, bf16[8,1,2,512]{3,0,2,1:T(8,128)(2,1)S(1)}, u32[]{:S(2)}, u32[]{:S(2)}) collective-permute-start(bf16[8,1,2,512]{3,0,2,1:T(8,128)(2,1)S(1)} %get-tuple-element.17), channel_id=1, source_target_pairs={{1,0},{2,1},{3,2},{5,4},{6,5},{7,6},{9,8},{10,9},{11,10},{13,12},{... | collective-permute-start | bytes 49160 | tf_op jit(solution)/shard_map/ppermute | solution.py:18
  74.4 0.0 copy-done.6
  74.4 0.7 fusion.28
  75.1 0.0 collective-permute-done.2
  75.1 2.6 %collective-permute-done.3 = bf16[8,1,2,512]{3,0,2,1:T(8,128)(2,1)S(1)} collective-permute-done((bf16[8,1,2,512]{3,0,2,1:T(8,128)(2,1)S(1)}, bf16[8,1,2,512]{3,0,2,1:T(8,128)(2,1)S(1)}, u32[]{:S(2)}, u32[]{:S(2)}) %collective-permute-start.3) | collective-permute-done | bytes 16416 | tf_op jit(solution)/shard_map/ppermute | solution.py:18
  77.7 3.7 %subtract_convert_fusion = (bf16[8,2,1,512]{3,0,2,1:T(8,128)(2,1)S(1)}, bf16[8,2,1,512]{3,0,2,1:T(8,128)(2,1)S(1)}) fusion(f32[8,4,2,512]{3,0,2,1:T(8,128)S(1)} %maximum_convert_fusion.1, f32[]{:T(128)} %bitcast.30, f32[]{:T(128)} %bitcast.29, f32[]{:T(128)} %bitcast.28, f32[]{:T(128)} %bitcast.15, f32[]{:T(128)} %bitcast.13, f32[]{:T(128)} %bitcast), kind=kLoop, calls=%fused_computation.31 | loop fusion | flops 196608 | bytes 229400 | tf_op jit(solution)/shard_map/convert.1
  81.5 0.6 fusion.29
  82.2 30.5 %all-gather = f32[32,2,512]{2,1,0:T(2,128)S(1)} all-gather(f32[4,2,512]{2,1,0:T(2,128)S(1)} %copy.37), channel_id=2, replica_groups=mesh['mode'=8,'row'=4] {'mode'}, dimensions={0}, use_global_device_ids=true | all-gather | bytes 147456 | tf_op jit(solution)/shard_map/all_gather | solution.py:145
  112.8 0.6 broadcast_multiply_fusion
  (24 shorter events, 0.4 us)
Async XLA Ops:
  0.6 3.7 %copy-start = (f32[7,2,512]{2,1,0:T(2,128)S(1)}, f32[7,2,512]{2,1,0:T(2,128)}, u32[]{:S(2)}) copy-start(f32[7,2,512]{2,1,0:T(2,128)} %param.12) | copy-start | bytes 86020
  0.6 2.8 %copy-start.1 = (bf16[2,512,512]{2,1,0:T(8,128)(2,1)S(1)}, bf16[2,512,512]{2,1,0:T(8,128)(2,1)}, u32[]{:S(2)}) copy-start(bf16[2,512,512]{2,1,0:T(8,128)(2,1)} %param.10) | copy-start | bytes 3145732
  0.7 3.6 %copy-start.3 = (bf16[8,2,2,512]{3,2,1,0:T(2,128)(2,1)S(1)}, bf16[8,2,2,512]{3,2,1,0:T(2,128)(2,1)}, u32[]{:S(2)}) copy-start(bf16[8,2,2,512]{3,2,1,0:T(2,128)(2,1)} %param.8) | copy-start | bytes 98308
  0.7 3.7 %copy-start.10 = (s32[4]{0:T(128)S(1)}, s32[4]{0:T(128)}, u32[]{:S(2)}) copy-start(s32[4]{0:T(128)} %param.13) | copy-start | bytes 52
  0.7 3.7 %copy-start.9 = (f32[4]{0:T(128)S(1)}, f32[4]{0:T(128)}, u32[]{:S(2)}) copy-start(f32[4]{0:T(128)} %param.14) | copy-start | bytes 52
  9.2 6.7 %copy-start.4 = (bf16[8,2,2,512]{3,2,1,0:T(2,128)(2,1)S(1)}, bf16[8,2,2,512]{3,2,1,0:T(2,128)(2,1)}, u32[]{:S(2)}) copy-start(bf16[8,2,2,512]{3,2,1,0:T(2,128)(2,1)} %param.9) | copy-start | bytes 98308
  9.2 38.6 %copy-start.8 = (s32[80,2]{0,1:T(2,128)S(1)}, s32[80,2]{0,1:T(2,128)}, u32[]{:S(2)}) copy-start(s32[80,2]{0,1:T(2,128)} %param.15) | copy-start | bytes 1924
  9.2 38.6 %copy-start.5 = (f32[2,3]{1,0:T(2,128)S(1)}, f32[2,3]{1,0:T(2,128)}, u32[]{:S(2)}) copy-start(f32[2,3]{1,0:T(2,128)} %param.11) | copy-start | bytes 76
  9.2 41.1 %copy-start.2 = (bf16[512,512]{0,1:T(8,128)(2,1)S(1)}, bf16[512,512]{0,1:T(8,128)(2,1)}, u32[]{:S(2)}) copy-start(bf16[512,512]{0,1:T(8,128)(2,1)} %get-tuple-element.6) | copy-start | bytes 1572868
  12.1 42.2 %collective-permute-start = (bf16[8,1,2,512]{3,0,2,1:T(8,128)(2,1)}, bf16[8,1,2,512]{3,0,2,1:T(8,128)(2,1)S(1)}, u32[]{:S(2)}, u32[]{:S(2)}) collective-permute-start(bf16[8,1,2,512]{3,0,2,1:T(8,128)(2,1)} %get-tuple-element.18), channel_id=1, source_target_pairs={{0,1},{1,2},{2,3},{4,5},{5,6},{6,7},{8,9},{9,10},{10,11},{12,13},{... | collective-permute-start | bytes 49160 | tf_op jit(solution)/shard_map/ppermute | solution.py:17
  14.5 39.8 %collective-permute-start.1 = (bf16[8,1,2,512]{3,0,2,1:T(8,128)(2,1)S(1)}, bf16[8,1,2,512]{3,0,2,1:T(8,128)(2,1)S(1)}, u32[]{:S(2)}, u32[]{:S(2)}) collective-permute-start(bf16[8,1,2,512]{3,0,2,1:T(8,128)(2,1)S(1)} %get-tuple-element.19), channel_id=1, source_target_pairs={{1,0},{2,1},{3,2},{5,4},{6,5},{7,6},{9,8},{10,9},{11,10},{13,12},{... | collective-permute-start | bytes 49160 | tf_op jit(solution)/shard_map/ppermute | solution.py:18
  51.7 18.1 %copy-start.7 = (f32[8,64]{1,0:T(8,128)S(1)}, f32[8,64]{1,0:T(8,128)}, u32[]{:S(2)}) copy-start(f32[8,64]{1,0:T(8,128)} %convolution_multiply_fusion.1) | copy-start | bytes 6148
  51.7 22.6 %copy-start.6 = (f32[1,3]{1,0:T(1,128)S(1)}, f32[1,3]{1,0:T(1,128)}, u32[]{:S(2)}) copy-start(f32[1,3]{1,0:T(1,128)} %slice_negate_fusion.1) | copy-start | bytes 40
  70.8 4.2 %collective-permute-start.2 = (bf16[8,1,2,512]{3,0,2,1:T(8,128)(2,1)S(1)}, bf16[8,1,2,512]{3,0,2,1:T(8,128)(2,1)S(1)}, u32[]{:S(2)}, u32[]{:S(2)}) collective-permute-start(bf16[8,1,2,512]{3,0,2,1:T(8,128)(2,1)S(1)} %get-tuple-element.16), channel_id=1, source_target_pairs={{0,1},{1,2},{2,3},{4,5},{5,6},{6,7},{8,9},{9,10},{10,11},{12,13},{... | collective-permute-start | bytes 49160 | tf_op jit(solution)/shard_map/ppermute | solution.py:17
  73.1 4.6 %collective-permute-start.3 = (bf16[8,1,2,512]{3,0,2,1:T(8,128)(2,1)S(1)}, bf16[8,1,2,512]{3,0,2,1:T(8,128)(2,1)S(1)}, u32[]{:S(2)}, u32[]{:S(2)}) collective-permute-start(bf16[8,1,2,512]{3,0,2,1:T(8,128)(2,1)S(1)} %get-tuple-element.17), channel_id=1, source_target_pairs={{1,0},{2,1},{3,2},{5,4},{6,5},{7,6},{9,8},{10,9},{11,10},{13,12},{... | collective-permute-start | bytes 49160 | tf_op jit(solution)/shard_map/ppermute | solution.py:18
